TPU v7x, 256 devices: a whole 4x4x8 slice. The times are simulated.
256 devices in a mesh: row: 16 (over z, core), col: 16 (over x, y).
Axes of the slice: x: 4, y: 4, z: 8, core: 2. Of those that a mesh axis runs over, the one named last changes fastest.
Arguments:
- work: float32 [8192, 8192], P('row', 'col'), may hold values from -6 to 6
- a_tiles: bfloat16 [16, 16, 512, 512], P('row', None, 'col'), may hold values from -0.078125 to 0.078125
- b_tiles: bfloat16 [16, 16, 512, 512], P(None, 'col', 'row'), may hold values from -0.078125 to 0.078125
- u_powers: float32 [16, 3, 512, 512], P('row', None, 'col'), may hold values from -1 to 1, as said below
- v_powers: float32 [16, 3, 512, 512], P('col', None, 'row'), may hold values from -1 to 1, as said below
- shift: float32 [1], replicated, may hold values from 0.5 to 2
Outputs:
- progress: float32 [8192, 8192], P('row', 'col')
Inputs may be any that keep to these rules, and one draw needn't show every extreme that they name: u_powers[i] holds U, U^2 and U^4 for a lower triangular U whose diagonal entries have magnitudes 0.3 to 0.9. v_powers[j] holds V, V^2 and V^4 for an upper triangular V whose diagonal entries have magnitudes 0.3 to 0.9.
All inputs are finite; a program needn't handle non-finite values.
Results may differ from a plain program's by a relative error of at most 0.0023.
Values may be sent and summed in bfloat16 or wider, within the bound.
No kernel may reach another device: no remote copies, remote signals or barrier semaphores. Data moves between devices by JAX's collectives and lax.ppermute only.
A program may use at most 128 MiB of HBM per device.

v0:
```python
import jax
import jax.numpy as jnp
import numpy as np
from jax import lax
from jax.sharding import PartitionSpec as P

FRONTS = 3
finest = lax.Precision.HIGHEST


def in_order(blocks, dim):
    blocks = jnp.moveaxis(blocks, 0, dim)
    shape = blocks.shape
    return blocks.reshape(*shape[:dim], shape[dim] * shape[dim + 1], *shape[dim + 2 :])


def from_everyone(array, axis):
    copies = jnp.broadcast_to(array, (lax.axis_size(axis), *array.shape))
    return lax.all_to_all(copies, axis, split_axis=0, concat_axis=0, tiled=True)


def gathered_copies(array, axis, dim):
    return in_order(from_everyone(array, axis), dim)


def broadcast(array, axis, root):
    return lax.dynamic_index_in_dim(lax.all_gather(array, axis), root, 0, keepdims=False)


def product(left_side, right_side):
    return jnp.dot(left_side, right_side, preferred_element_type=jnp.float32, precision=finest)


def keep(source):
    return source


def per_device(work, a_tiles, b_tiles, u_powers, v_powers, shift):
    rows_count = lax.axis_size("row")
    cols_count = lax.axis_size("col")
    my_row = lax.axis_index("row")
    my_col = lax.axis_index("col")
    my_front = my_row + my_col
    first = max(0, (rows_count + cols_count) // 2 - FRONTS)
    width = work.shape[0]
    identity = jnp.eye(width, dtype=jnp.float32)
    shift_value = shift[0]
    u_base = gathered_copies(u_powers[:, :1], "col", 2)[0, 0]
    v_base = lax.all_gather(v_powers[:, :1], "row", axis=2, tiled=True)[0, 0]

    def powers_of():
        u_square = product(u_base, u_base)
        v_square = product(v_base, v_base)
        return (
            [u_base, u_square, product(u_square, u_square)],
            [v_base, v_square, product(v_square, v_square)],
        )

    def solve(source):
        u_list, v_list = powers_of()
        current = product(product(identity - u_list[0], source), identity - v_list[0]) / (
            2.0 * shift_value
        )
        for power in range(3):
            current = current + product(product(u_list[power], current), v_list[power])
        return current

    current = work
    for number in range(FRONTS):
        front = first + number
        current = lax.cond(my_front == front, solve, keep, current)
        sent = current.astype(jnp.bfloat16)
        down_row = front - my_col
        across_col = front - my_row
        valid_down = (down_row >= 0) & (down_row < rows_count)
        valid_across = (across_col >= 0) & (across_col < cols_count)
        down_clip = jnp.clip(down_row, 0, rows_count - 1)
        across_clip = jnp.clip(across_col, 0, cols_count - 1)
        down_tile = broadcast(sent, "row", down_clip)
        across_tile = broadcast(sent, "col", across_clip)
        a_rows = np.clip(front - np.arange(cols_count), 0, rows_count - 1).astype(np.int32)
        b_rows = np.clip(front - np.arange(rows_count), 0, cols_count - 1).astype(np.int32)
        a_tile = lax.all_to_all(
            a_tiles[0, a_rows], "col", split_axis=0, concat_axis=0, tiled=True
        ).reshape(width, width)
        b_tile = lax.all_to_all(
            b_tiles[b_rows, 0], "row", split_axis=0, concat_axis=0, tiled=True
        ).reshape(width, width)

        def update(source):
            minus_a = jnp.dot(a_tile, down_tile, preferred_element_type=jnp.float32)
            minus_b = jnp.dot(across_tile, b_tile, preferred_element_type=jnp.float32)
            return (
                source - jnp.where(valid_down, minus_a, 0.0) - jnp.where(valid_across, minus_b, 0.0)
            )

        current = lax.cond(my_front > front, update, keep, current)
    return current


def solution(mesh):
    placed = (
        P("row", "col"),
        P("row", None, "col", None),
        P(None, "col", "row", None),
        P("row", None, "col", None),
        P("col", None, "row", None),
        P(),
    )
    return jax.shard_map(
        per_device, mesh=mesh, in_specs=placed, out_specs=P("row", "col"), check_vma=False
    )
```

profile of v0, /device:TPU:70, one launch (start us, length us, event | category | flops | bytes accessed | tf_op | source)
XLA Modules:
  0.0 593.5 jit_solution(3004908231699741183)
XLA Ops:
  12.3 7.4 %all-to-all-start = ((f32[16,1,1,32,512]{4,3,2,1,0:T(8,128)}), f32[16,1,1,32,512]{4,3,2,1,0:T(8,128)S(1)}, u32[]{:S(2)}, u32[]{:S(2)}) async-start(f32[16,1,1,32,512]{4,3,2,1,0:T(8,128)} %broadcast_in_dim.35), calls=%async_computation | async-start | bytes 2097152 | tf_op jit(solution)/shard_map/all_to_all | solution.py:19
  20.9 14.1 %all-to-all-done = f32[16,1,1,32,512]{4,3,2,1,0:T(8,128)S(1)} async-done(((f32[16,1,1,32,512]{4,3,2,1,0:T(8,128)}), f32[16,1,1,32,512]{4,3,2,1,0:T(8,128)S(1)}, u32[]{:S(2)}, u32[]{:S(2)}) %all-to-all-start) | async-done | bytes 1048608 | tf_op jit(solution)/shard_map/all_to_all | solution.py:19
  35.0 14.5 %all-gather.14.cloned.1.call-done = f32[1,1,512,512]{3,2,1,0:T(8,128)} async-done(((f32[1,1,32,512]{3,2,1,0:T(8,128)}), f32[1,1,512,512]{3,2,1,0:T(8,128)}) %all-gather.14.cloned.1.call-update) | async-done | bytes 1048592 | tf_op jit(solution)/shard_map/all_gather | solution.py:49
  56.7 33.7 %all-to-all-start.1 = ((bf16[16,32,512]{2,1,0:T(8,128)(2,1)}), bf16[16,32,512]{2,1,0:T(8,128)(2,1)}, u32[]{:S(2)}, u32[]{:S(2)}) async-start(bf16[16,32,512]{2,1,0:T(8,128)(2,1)} %gather_fusion), calls=%async_computation.1 | async-start | bytes 1048576 | tf_op jit(solution)/shard_map/all_to_all | solution.py:83
  91.8 8.6 %all-to-all-done.1 = bf16[16,32,512]{2,1,0:T(8,128)(2,1)} async-done(((bf16[16,32,512]{2,1,0:T(8,128)(2,1)}), bf16[16,32,512]{2,1,0:T(8,128)(2,1)}, u32[]{:S(2)}, u32[]{:S(2)}) %all-to-all-start.1) | async-done | bytes 524320 | tf_op jit(solution)/shard_map/all_to_all | solution.py:83
  100.4 10.2 %all-to-all-start.2 = ((bf16[16,32,512]{2,1,0:T(8,128)(2,1)}), bf16[16,32,512]{2,1,0:T(8,128)(2,1)}, u32[]{:S(2)}, u32[]{:S(2)}) async-start(bf16[16,32,512]{2,1,0:T(8,128)(2,1)} %gather_fusion.1), calls=%async_computation.2 | async-start | bytes 1048576 | tf_op jit(solution)/shard_map/all_to_all | solution.py:86
  110.6 14.9 %all-to-all-done.2 = bf16[16,32,512]{2,1,0:T(8,128)(2,1)} async-done(((bf16[16,32,512]{2,1,0:T(8,128)(2,1)}), bf16[16,32,512]{2,1,0:T(8,128)(2,1)}, u32[]{:S(2)}, u32[]{:S(2)}) %all-to-all-start.2) | async-done | bytes 524320 | tf_op jit(solution)/shard_map/all_to_all | solution.py:86
  125.5 31.5 %all-gather.18.cloned.1.call-done = bf16[8192,512]{1,0:T(8,128)(2,1)} async-done(((bf16[512,512]{1,0:T(8,128)(2,1)}), bf16[8192,512]{1,0:T(8,128)(2,1)}) %all-gather.18.cloned.1.call-update) | async-done | bytes 8388624 | tf_op jit(solution)/shard_map/all_gather | solution.py:27
  156.9 55.6 %all-gather.16.cloned.1.call-done = bf16[8192,512]{1,0:T(8,128)(2,1)} async-done(((bf16[512,512]{1,0:T(8,128)(2,1)}), bf16[8192,512]{1,0:T(8,128)(2,1)}) %all-gather.16.cloned.1.call-update) | async-done | bytes 8388624 | tf_op jit(solution)/shard_map/all_gather | solution.py:27
  212.6 8.5 %conditional.7 = (f32[512,512]{0,1:T(8,128)}) conditional(s32[]{:T(128)} %convert_element_type.44, (f32[512,512]{1,0:T(8,128)}) %conditional.6, (s32[]{:T(128)}, bf16[16,32,512]{2,1,0:T(8,128)(2,1)}, bf16[16,512,512]{2,1,0:T(8,128)(2,1)}, f32[512,512]{1,0:T(8,128)}, s32[]{:T(128)}, /*index=5*/bf16[16,512,512]{2,1,0:T(8,128)(2,1)}, ...), branch_computations={%region_2.3_spmd, %region_3.4_spmd.clone} | conditional | flops 537919488 | bytes 8388740 | solution.py:97
  230.4 32.5 %all-to-all-start.3 = ((bf16[16,32,512]{2,1,0:T(8,128)(2,1)}), bf16[16,32,512]{2,1,0:T(8,128)(2,1)}, u32[]{:S(2)}, u32[]{:S(2)}) async-start(bf16[16,32,512]{2,1,0:T(8,128)(2,1)} %gather_fusion.2), calls=%async_computation.3 | async-start | bytes 1048576 | tf_op jit(solution)/shard_map/all_to_all | solution.py:83
  264.3 7.1 %all-to-all-done.3 = bf16[16,32,512]{2,1,0:T(8,128)(2,1)} async-done(((bf16[16,32,512]{2,1,0:T(8,128)(2,1)}), bf16[16,32,512]{2,1,0:T(8,128)(2,1)}, u32[]{:S(2)}, u32[]{:S(2)}) %all-to-all-start.3) | async-done | bytes 524320 | tf_op jit(solution)/shard_map/all_to_all | solution.py:83
  271.3 6.3 %all-to-all-start.4 = ((bf16[16,32,512]{2,1,0:T(8,128)(2,1)}), bf16[16,32,512]{2,1,0:T(8,128)(2,1)}, u32[]{:S(2)}, u32[]{:S(2)}) async-start(bf16[16,32,512]{2,1,0:T(8,128)(2,1)} %gather_fusion.3), calls=%async_computation.4 | async-start | bytes 1048576 | tf_op jit(solution)/shard_map/all_to_all | solution.py:86
  277.6 19.4 %all-to-all-done.4 = bf16[16,32,512]{2,1,0:T(8,128)(2,1)} async-done(((bf16[16,32,512]{2,1,0:T(8,128)(2,1)}), bf16[16,32,512]{2,1,0:T(8,128)(2,1)}, u32[]{:S(2)}, u32[]{:S(2)}) %all-to-all-start.4) | async-done | bytes 524320 | tf_op jit(solution)/shard_map/all_to_all | solution.py:86
  297.0 20.9 %all-gather.20.cloned.1.call-done = bf16[8192,512]{1,0:T(8,128)(2,1)} async-done(((bf16[512,512]{1,0:T(8,128)(2,1)}), bf16[8192,512]{1,0:T(8,128)(2,1)}) %all-gather.20.cloned.1.call-update) | async-done | bytes 8388624 | tf_op jit(solution)/shard_map/all_gather | solution.py:27
  317.9 78.5 %all-gather.22.cloned.1.call-done = bf16[8192,512]{1,0:T(8,128)(2,1)} async-done(((bf16[512,512]{1,0:T(8,128)(2,1)}), bf16[8192,512]{1,0:T(8,128)(2,1)}) %all-gather.22.cloned.1.call-update) | async-done | bytes 8388624 | tf_op jit(solution)/shard_map/all_gather | solution.py:27
  396.4 8.5 %conditional.9 = (f32[512,512]{0,1:T(8,128)}) conditional(s32[]{:T(128)} %convert_element_type.42, (f32[512,512]{1,0:T(8,128)}) %conditional.8, (s32[]{:T(128)}, bf16[16,32,512]{2,1,0:T(8,128)(2,1)}, bf16[16,512,512]{2,1,0:T(8,128)(2,1)}, f32[512,512]{1,0:T(8,128)}, s32[]{:T(128)}, /*index=5*/bf16[16,512,512]{2,1,0:T(8,128)(2,1)}, ...), branch_computations={%region_6.7_spmd, %region_7.8_spmd.clone} | conditional | flops 537919488 | bytes 8388740 | solution.py:97
  412.3 30.6 %all-to-all-start.5 = ((bf16[16,32,512]{2,1,0:T(8,128)(2,1)}), bf16[16,32,512]{2,1,0:T(8,128)(2,1)S(1)}, u32[]{:S(2)}, u32[]{:S(2)}) async-start(bf16[16,32,512]{2,1,0:T(8,128)(2,1)} %gather_fusion.4), calls=%async_computation.5 | async-start | bytes 1048576 | tf_op jit(solution)/shard_map/all_to_all | solution.py:83
  444.2 8.2 %all-to-all-done.5 = bf16[16,32,512]{2,1,0:T(8,128)(2,1)S(1)} async-done(((bf16[16,32,512]{2,1,0:T(8,128)(2,1)}), bf16[16,32,512]{2,1,0:T(8,128)(2,1)S(1)}, u32[]{:S(2)}, u32[]{:S(2)}) %all-to-all-start.5) | async-done | bytes 524320 | tf_op jit(solution)/shard_map/all_to_all | solution.py:83
  452.4 6.2 %all-to-all-start.6 = ((bf16[16,32,512]{2,1,0:T(8,128)(2,1)}), bf16[16,32,512]{2,1,0:T(8,128)(2,1)S(1)}, u32[]{:S(2)}, u32[]{:S(2)}) async-start(bf16[16,32,512]{2,1,0:T(8,128)(2,1)} %gather_fusion.5), calls=%async_computation.6 | async-start | bytes 1048576 | tf_op jit(solution)/shard_map/all_to_all | solution.py:86
  458.6 19.4 %all-to-all-done.6 = bf16[16,32,512]{2,1,0:T(8,128)(2,1)S(1)} async-done(((bf16[16,32,512]{2,1,0:T(8,128)(2,1)}), bf16[16,32,512]{2,1,0:T(8,128)(2,1)S(1)}, u32[]{:S(2)}, u32[]{:S(2)}) %all-to-all-start.6) | async-done | bytes 524320 | tf_op jit(solution)/shard_map/all_to_all | solution.py:86
  477.9 21.0 %all-gather.24.cloned.1.call-done = bf16[8192,512]{1,0:T(8,128)(2,1)} async-done(((bf16[512,512]{1,0:T(8,128)(2,1)}), bf16[8192,512]{1,0:T(8,128)(2,1)}) %all-gather.24.cloned.1.call-update) | async-done | bytes 8388624 | tf_op jit(solution)/shard_map/all_gather | solution.py:27
  498.9 78.6 %all-gather.26.cloned.1.call-done = bf16[8192,512]{1,0:T(8,128)(2,1)} async-done(((bf16[512,512]{1,0:T(8,128)(2,1)}), bf16[8192,512]{1,0:T(8,128)(2,1)}) %all-gather.26.cloned.1.call-update) | async-done | bytes 8388624 | tf_op jit(solution)/shard_map/all_gather | solution.py:27
  577.6 6.1 %conditional.11 = (f32[512,512]{0,1:T(8,128)}) conditional(s32[]{:T(128)} %convert_element_type.40, (f32[512,512]{1,0:T(8,128)S(1)}) %conditional.10, (s32[]{:T(128)}, bf16[16,512,512]{2,1,0:T(8,128)(2,1)}, bf16[16,32,512]{2,1,0:T(8,128)(2,1)S(1)}, f32[512,512]{1,0:T(8,128)S(1)}, s32[]{:T(128)}, /*index=5*/bf16[16,512,512]{2,1,0:T(8,128)(2,1)}, ...), branch_computations={%region_10.11_spmd, %region_11.12_spmd} | conditional | flops 537919488 | bytes 10485920 | solution.py:97
  (57 shorter events, 64.5 us)
Async XLA Ops:
  6.5 48.8 %copy-start = (bf16[1,16,32,512]{3,2,1,0:T(8,128)(2,1)S(1)}, bf16[1,16,32,512]{3,2,1,0:T(8,128)(2,1)}, u32[]{:S(2)}) copy-start(bf16[1,16,32,512]{3,2,1,0:T(8,128)(2,1)} %param.31) | copy-start | bytes 1572868
  6.5 43.0 %all-gather.14.cloned.1.call-start = ((), (), s32[]{:S(2)}) async-start(), calls=%async_computation.7 | async-start | bytes 1114112 | tf_op jit(solution)/shard_map/all_gather | solution.py:49
  12.3 22.7 %all-to-all-start = ((f32[16,1,1,32,512]{4,3,2,1,0:T(8,128)}), f32[16,1,1,32,512]{4,3,2,1,0:T(8,128)S(1)}, u32[]{:S(2)}, u32[]{:S(2)}) async-start(f32[16,1,1,32,512]{4,3,2,1,0:T(8,128)} %broadcast_in_dim.35), calls=%async_computation | async-start | bytes 2097152 | tf_op jit(solution)/shard_map/all_to_all | solution.py:19
  19.8 137.2 %all-gather.18.cloned.1.call-start = ((), (), s32[]{:S(2)}) async-start(), calls=%async_computation.9 | async-start | bytes 8912896 | tf_op jit(solution)/shard_map/all_gather | solution.py:27
  49.5 5.8 copy-start.7
  49.5 40.9 %copy-start.3 = (bf16[16,1,32,512]{3,2,1,0:T(8,128)(2,1)S(1)}, bf16[16,1,32,512]{3,2,1,0:T(8,128)(2,1)}, u32[]{:S(2)}) copy-start(bf16[16,1,32,512]{3,2,1,0:T(8,128)(2,1)} %param.32) | copy-start | bytes 1572868
  52.4 168.7 %copy-start.1 = (f32[1,1,512,512]{3,2,1,0:T(8,128)S(1)}, f32[1,1,512,512]{3,2,1,0:T(8,128)}, u32[]{:S(2)}) copy-start(f32[1,1,512,512]{3,2,1,0:T(8,128)} %all-gather.14.cloned.1.call-done) | copy-start | bytes 3145732
  54.6 158.0 %all-gather.16.cloned.1.call-start = ((), (), s32[]{:S(2)}) async-start(), calls=%async_computation.8 | async-start | bytes 8912896 | tf_op jit(solution)/shard_map/all_gather | solution.py:27
  56.7 43.7 %all-to-all-start.1 = ((bf16[16,32,512]{2,1,0:T(8,128)(2,1)}), bf16[16,32,512]{2,1,0:T(8,128)(2,1)}, u32[]{:S(2)}, u32[]{:S(2)}) async-start(bf16[16,32,512]{2,1,0:T(8,128)(2,1)} %gather_fusion), calls=%async_computation.1 | async-start | bytes 1048576 | tf_op jit(solution)/shard_map/all_to_all | solution.py:83
  100.4 25.1 %all-to-all-start.2 = ((bf16[16,32,512]{2,1,0:T(8,128)(2,1)}), bf16[16,32,512]{2,1,0:T(8,128)(2,1)}, u32[]{:S(2)}, u32[]{:S(2)}) async-start(bf16[16,32,512]{2,1,0:T(8,128)(2,1)} %gather_fusion.1), calls=%async_computation.2 | async-start | bytes 1048576 | tf_op jit(solution)/shard_map/all_to_all | solution.py:86
  110.6 207.4 %all-gather.20.cloned.1.call-start = ((), (), s32[]{:S(2)}) async-start(), calls=%async_computation.10 | async-start | bytes 8912896 | tf_op jit(solution)/shard_map/all_gather | solution.py:27
  221.1 7.9 %copy-start.6 = (s32[16]{0:T(128)S(1)}, s32[16]{0:T(128)}, u32[]{:S(2)}) copy-start(s32[16]{0:T(128)} %constant.202) | copy-start | bytes 196
  228.4 168.0 %all-gather.22.cloned.1.call-start = ((), (), s32[]{:S(2)}) async-start(), calls=%async_computation.11 | async-start | bytes 8912896 | tf_op jit(solution)/shard_map/all_gather | solution.py:27
  230.4 40.9 %all-to-all-start.3 = ((bf16[16,32,512]{2,1,0:T(8,128)(2,1)}), bf16[16,32,512]{2,1,0:T(8,128)(2,1)}, u32[]{:S(2)}, u32[]{:S(2)}) async-start(bf16[16,32,512]{2,1,0:T(8,128)(2,1)} %gather_fusion.2), calls=%async_computation.3 | async-start | bytes 1048576 | tf_op jit(solution)/shard_map/all_to_all | solution.py:83
  271.3 25.7 %all-to-all-start.4 = ((bf16[16,32,512]{2,1,0:T(8,128)(2,1)}), bf16[16,32,512]{2,1,0:T(8,128)(2,1)}, u32[]{:S(2)}, u32[]{:S(2)}) async-start(bf16[16,32,512]{2,1,0:T(8,128)(2,1)} %gather_fusion.3), calls=%async_computation.4 | async-start | bytes 1048576 | tf_op jit(solution)/shard_map/all_to_all | solution.py:86
  277.6 221.3 %all-gather.24.cloned.1.call-start = ((), (), s32[]{:S(2)}) async-start(), calls=%async_computation.12 | async-start | bytes 8912896 | tf_op jit(solution)/shard_map/all_gather | solution.py:27
  404.9 5.9 %copy-start.5 = (s32[16]{0:T(128)S(1)}, s32[16]{0:T(128)}, u32[]{:S(2)}) copy-start(s32[16]{0:T(128)} %constant.218) | copy-start | bytes 196
  410.1 167.4 %all-gather.26.cloned.1.call-start = ((), (), s32[]{:S(2)}) async-start(), calls=%async_computation.13 | async-start | bytes 8912896 | tf_op jit(solution)/shard_map/all_gather | solution.py:27
  412.3 40.1 %all-to-all-start.5 = ((bf16[16,32,512]{2,1,0:T(8,128)(2,1)}), bf16[16,32,512]{2,1,0:T(8,128)(2,1)S(1)}, u32[]{:S(2)}, u32[]{:S(2)}) async-start(bf16[16,32,512]{2,1,0:T(8,128)(2,1)} %gather_fusion.4), calls=%async_computation.5 | async-start | bytes 1048576 | tf_op jit(solution)/shard_map/all_to_all | solution.py:83
  452.4 25.5 %all-to-all-start.6 = ((bf16[16,32,512]{2,1,0:T(8,128)(2,1)}), bf16[16,32,512]{2,1,0:T(8,128)(2,1)S(1)}, u32[]{:S(2)}, u32[]{:S(2)}) async-start(bf16[16,32,512]{2,1,0:T(8,128)(2,1)} %gather_fusion.5), calls=%async_computation.6 | async-start | bytes 1048576 | tf_op jit(solution)/shard_map/all_to_all | solution.py:86
  577.6 2.7 copy-start.4
Sparse Core Ops, SparseCore 0:
  10.5 38.9 all-gather.13
  54.7 102.1 all-gather.17
  158.8 53.7 all-gather.15
  228.5 89.3 all-gather.19
  320.2 76.1 all-gather.21
  410.2 88.6 all-gather.23
  501.3 76.1 all-gather.25
where the time goes:
time: 604 us; the launch traced here: 594 us
  waiting for transfers between devices  394 us (65%)
  starting transfers between devices  127 us (21%)
  local copies, waits for them, and re-layouts  26.1 us (4%)
  matrix products  17.7 us (3%)
  between operations  14.1 us (2%)
  loops' own time  8.24 us (1%)
  other arithmetic  6.23 us (1%)
    all_gather x6, waiting for transfers between devices, broadcast(): lax.all_gather(array, axis)  286 us
    all_to_all x3, starting transfers between devices, per_device(): lax.all_to_all(a_tiles[0, a_rows], 'col', split_axis=0, concat_axis=0, ti...  96.8 us
    all_to_all x3, waiting for transfers between devices, per_device(): lax.all_to_all(b_tiles[b_rows, 0], 'row', split_axis=0, concat_axis=0, ti...  53.6 us
    all_to_all x3, waiting for transfers between devices, per_device(): lax.all_to_all(a_tiles[0, a_rows], 'col', split_axis=0, concat_axis=0, ti...  23.9 us
    all_to_all x3, starting transfers between devices, per_device(): lax.all_to_all(b_tiles[b_rows, 0], 'row', split_axis=0, concat_axis=0, ti...  22.6 us
    all_gather x1, waiting for transfers between devices, per_device(): v_base = lax.all_gather(v_powers[:, :1], 'row', axis=2, tiled=True)[0, 0]  14.5 us
    all_to_all x1, waiting for transfers between devices, from_everyone(): return lax.all_to_all(copies, axis, split_axis=0, concat_axis=0, tiled=True)  14.1 us
  transfers between devices with their start and end apart: 14, of which 14 were waited for; matrix products, arithmetic and copies ran while one was open for 2% of the time, Pallas kernels for 0%

commit v1 on v0

--- a/solution.py
+++ b/solution.py
@@ -6,6 +6,13 @@
 
 FRONTS = 3
 finest = lax.Precision.HIGHEST
+
+
+def all_by_exchange(shard, name, dim):
+    peers = lax.axis_size(name)
+    blocks = jnp.stack([shard for _ in range(peers)])
+    blocks = lax.all_to_all(blocks, name, split_axis=0, concat_axis=0)
+    return jnp.concatenate(blocks, axis=dim)
 
 
 def in_order(blocks, dim):
@@ -46,7 +53,7 @@
     identity = jnp.eye(width, dtype=jnp.float32)
     shift_value = shift[0]
     u_base = gathered_copies(u_powers[:, :1], "col", 2)[0, 0]
-    v_base = lax.all_gather(v_powers[:, :1], "row", axis=2, tiled=True)[0, 0]
+    v_base = all_by_exchange(v_powers[:, :1], "row", 2)[0, 0]
 
     def powers_of():
         u_square = product(u_base, u_base)

time: 604 us -> 632 us (1.046)
  waiting for transfers between devices: 394 us -> 421 us
    all_to_all x0 -> x1, waiting for transfers between devices: none -> 23.2 us  [all_by_exchange(): blocks = lax.all_to_all(blocks, name, split_axis=0, concat_axis=0)]
    all_gather x1 -> x0, waiting for transfers between devices: 14.5 us -> none  [per_device(): v_base = lax.all_gather(v_powers[:, :1], 'row', axis=2, tiled=True)[0, 0]]
    all_gather x6, waiting for transfers between devices: 286 us -> 299 us  [broadcast(): lax.all_gather(array, axis)]
    all_to_all x0 -> x1, starting transfers between devices: none -> 8.13 us  [all_by_exchange(): blocks = lax.all_to_all(blocks, name, split_axis=0, concat_axis=0)]
where the time goes in v1:
time: 632 us; the launch traced here: 622 us
  waiting for transfers between devices  421 us (67%)
  starting transfers between devices  128 us (20%)
  local copies, waits for them, and re-layouts  26.5 us (4%)
  matrix products  17.7 us (3%)
  between operations  14.1 us (2%)
  loops' own time  8.23 us (1%)
    all_gather x6, waiting for transfers between devices, broadcast(): lax.all_gather(array, axis)  299 us
    all_to_all x3, starting transfers between devices, per_device(): lax.all_to_all(a_tiles[0, a_rows], 'col', split_axis=0, concat_axis=0, ti...  93.4 us
    all_to_all x3, waiting for transfers between devices, per_device(): lax.all_to_all(b_tiles[b_rows, 0], 'row', split_axis=0, concat_axis=0, ti...  58.1 us
    all_to_all x3, waiting for transfers between devices, per_device(): lax.all_to_all(a_tiles[0, a_rows], 'col', split_axis=0, concat_axis=0, ti...  24.3 us
    all_to_all x1, waiting for transfers between devices, all_by_exchange(): blocks = lax.all_to_all(blocks, name, split_axis=0, concat_axis=0)  23.2 us
    all_to_all x3, starting transfers between devices, per_device(): lax.all_to_all(b_tiles[b_rows, 0], 'row', split_axis=0, concat_axis=0, ti...  19 us
    all_to_all x1, waiting for transfers between devices, from_everyone(): return lax.all_to_all(copies, axis, split_axis=0, concat_axis=0, tiled=True)  14.4 us
  transfers between devices with their start and end apart: 14, of which 14 were waited for; matrix products, arithmetic and copies ran while one was open for 2% of the time, Pallas kernels for 0%

profile of v1, /device:TPU:70, one launch (start us, length us, event | category | flops | bytes accessed | tf_op | source)
XLA Modules:
  0.0 621.9 jit_solution(12713741745803219165)
XLA Ops:
  10.8 7.4 %all-to-all-start = ((f32[16,1,1,32,512]{4,3,2,1,0:T(8,128)}), f32[16,1,1,32,512]{4,3,2,1,0:T(8,128)S(1)}, u32[]{:S(2)}, u32[]{:S(2)}) async-start(f32[16,1,1,32,512]{4,3,2,1,0:T(8,128)} %broadcast_in_dim.35), calls=%async_computation | async-start | bytes 2097152 | tf_op jit(solution)/shard_map/all_to_all | solution.py:26
  19.1 14.4 %all-to-all-done = f32[16,1,1,32,512]{4,3,2,1,0:T(8,128)S(1)} async-done(((f32[16,1,1,32,512]{4,3,2,1,0:T(8,128)}), f32[16,1,1,32,512]{4,3,2,1,0:T(8,128)S(1)}, u32[]{:S(2)}, u32[]{:S(2)}) %all-to-all-start) | async-done | bytes 1048608 | tf_op jit(solution)/shard_map/all_to_all | solution.py:26
  34.6 8.1 %all-to-all-start.1 = ((f32[16,1,1,32,512]{4,3,2,1,0:T(8,128)}), f32[16,1,1,32,512]{4,3,2,1,0:T(8,128)S(1)}, u32[]{:S(2)}, u32[]{:S(2)}) async-start(f32[16,1,1,32,512]{4,3,2,1,0:T(8,128)} %stack.2), calls=%async_computation.1 | async-start | bytes 2097152 | tf_op jit(solution)/shard_map/all_to_all | solution.py:14
  43.9 23.2 %all-to-all-done.1 = f32[16,1,1,32,512]{4,3,2,1,0:T(8,128)S(1)} async-done(((f32[16,1,1,32,512]{4,3,2,1,0:T(8,128)}), f32[16,1,1,32,512]{4,3,2,1,0:T(8,128)S(1)}, u32[]{:S(2)}, u32[]{:S(2)}) %all-to-all-start.1) | async-done | bytes 1048608 | tf_op jit(solution)/shard_map/all_to_all | solution.py:14
  74.3 31.9 %all-to-all-start.2 = ((bf16[16,32,512]{2,1,0:T(8,128)(2,1)}), bf16[16,32,512]{2,1,0:T(8,128)(2,1)}, u32[]{:S(2)}, u32[]{:S(2)}) async-start(bf16[16,32,512]{2,1,0:T(8,128)(2,1)} %gather_fusion), calls=%async_computation.2 | async-start | bytes 1048576 | tf_op jit(solution)/shard_map/all_to_all | solution.py:90
  107.6 9.4 %all-to-all-done.2 = bf16[16,32,512]{2,1,0:T(8,128)(2,1)} async-done(((bf16[16,32,512]{2,1,0:T(8,128)(2,1)}), bf16[16,32,512]{2,1,0:T(8,128)(2,1)}, u32[]{:S(2)}, u32[]{:S(2)}) %all-to-all-start.2) | async-done | bytes 524320 | tf_op jit(solution)/shard_map/all_to_all | solution.py:90
  116.9 6.1 all-to-all-start.3
  123.1 19.4 %all-to-all-done.3 = bf16[16,32,512]{2,1,0:T(8,128)(2,1)} async-done(((bf16[16,32,512]{2,1,0:T(8,128)(2,1)}), bf16[16,32,512]{2,1,0:T(8,128)(2,1)}, u32[]{:S(2)}, u32[]{:S(2)}) %all-to-all-start.3) | async-done | bytes 524320 | tf_op jit(solution)/shard_map/all_to_all | solution.py:93
  142.4 20.4 %all-gather.13.cloned.1.call-done = bf16[8192,512]{1,0:T(8,128)(2,1)} async-done(((bf16[512,512]{1,0:T(8,128)(2,1)}), bf16[8192,512]{1,0:T(8,128)(2,1)}) %all-gather.13.cloned.1.call-update) | async-done | bytes 8388624 | tf_op jit(solution)/shard_map/all_gather | solution.py:34
  162.8 78.6 %all-gather.15.cloned.1.call-done = bf16[8192,512]{1,0:T(8,128)(2,1)} async-done(((bf16[512,512]{1,0:T(8,128)(2,1)}), bf16[8192,512]{1,0:T(8,128)(2,1)}) %all-gather.15.cloned.1.call-update) | async-done | bytes 8388624 | tf_op jit(solution)/shard_map/all_gather | solution.py:34
  241.4 8.5 %conditional.7 = (f32[512,512]{0,1:T(8,128)}) conditional(s32[]{:T(128)} %convert_element_type.44, (f32[512,512]{1,0:T(8,128)}) %conditional.6, (s32[]{:T(128)}, bf16[16,32,512]{2,1,0:T(8,128)(2,1)}, bf16[16,512,512]{2,1,0:T(8,128)(2,1)}, f32[512,512]{1,0:T(8,128)}, s32[]{:T(128)}, /*index=5*/bf16[16,512,512]{2,1,0:T(8,128)(2,1)}, ...), branch_computations={%region_2.3_spmd, %region_3.4_spmd.clone} | conditional | flops 537919488 | bytes 8388740 | solution.py:104
  259.3 31.0 %all-to-all-start.4 = ((bf16[16,32,512]{2,1,0:T(8,128)(2,1)}), bf16[16,32,512]{2,1,0:T(8,128)(2,1)}, u32[]{:S(2)}, u32[]{:S(2)}) async-start(bf16[16,32,512]{2,1,0:T(8,128)(2,1)} %gather_fusion.2), calls=%async_computation.4 | async-start | bytes 1048576 | tf_op jit(solution)/shard_map/all_to_all | solution.py:90
  291.6 6.8 %all-to-all-done.4 = bf16[16,32,512]{2,1,0:T(8,128)(2,1)} async-done(((bf16[16,32,512]{2,1,0:T(8,128)(2,1)}), bf16[16,32,512]{2,1,0:T(8,128)(2,1)}, u32[]{:S(2)}, u32[]{:S(2)}) %all-to-all-start.4) | async-done | bytes 524320 | tf_op jit(solution)/shard_map/all_to_all | solution.py:90
  298.4 6.7 %all-to-all-start.5 = ((bf16[16,32,512]{2,1,0:T(8,128)(2,1)}), bf16[16,32,512]{2,1,0:T(8,128)(2,1)}, u32[]{:S(2)}, u32[]{:S(2)}) async-start(bf16[16,32,512]{2,1,0:T(8,128)(2,1)} %gather_fusion.3), calls=%async_computation.5 | async-start | bytes 1048576 | tf_op jit(solution)/shard_map/all_to_all | solution.py:93
  305.2 19.4 %all-to-all-done.5 = bf16[16,32,512]{2,1,0:T(8,128)(2,1)} async-done(((bf16[16,32,512]{2,1,0:T(8,128)(2,1)}), bf16[16,32,512]{2,1,0:T(8,128)(2,1)}, u32[]{:S(2)}, u32[]{:S(2)}) %all-to-all-start.5) | async-done | bytes 524320 | tf_op jit(solution)/shard_map/all_to_all | solution.py:93
  324.6 21.9 %all-gather.17.cloned.1.call-done = bf16[8192,512]{1,0:T(8,128)(2,1)} async-done(((bf16[512,512]{1,0:T(8,128)(2,1)}), bf16[8192,512]{1,0:T(8,128)(2,1)}) %all-gather.17.cloned.1.call-update) | async-done | bytes 8388624 | tf_op jit(solution)/shard_map/all_gather | solution.py:34
  346.5 78.5 %all-gather.19.cloned.1.call-done = bf16[8192,512]{1,0:T(8,128)(2,1)} async-done(((bf16[512,512]{1,0:T(8,128)(2,1)}), bf16[8192,512]{1,0:T(8,128)(2,1)}) %all-gather.19.cloned.1.call-update) | async-done | bytes 8388624 | tf_op jit(solution)/shard_map/all_gather | solution.py:34
  425.0 8.5 %conditional.9 = (f32[512,512]{0,1:T(8,128)}) conditional(s32[]{:T(128)} %convert_element_type.42, (f32[512,512]{1,0:T(8,128)}) %conditional.8, (s32[]{:T(128)}, bf16[16,32,512]{2,1,0:T(8,128)(2,1)}, bf16[16,512,512]{2,1,0:T(8,128)(2,1)}, f32[512,512]{1,0:T(8,128)}, s32[]{:T(128)}, /*index=5*/bf16[16,512,512]{2,1,0:T(8,128)(2,1)}, ...), branch_computations={%region_6.7_spmd, %region_7.8_spmd.clone} | conditional | flops 537919488 | bytes 8388740 | solution.py:104
  440.7 30.6 %all-to-all-start.6 = ((bf16[16,32,512]{2,1,0:T(8,128)(2,1)}), bf16[16,32,512]{2,1,0:T(8,128)(2,1)S(1)}, u32[]{:S(2)}, u32[]{:S(2)}) async-start(bf16[16,32,512]{2,1,0:T(8,128)(2,1)} %gather_fusion.4), calls=%async_computation.6 | async-start | bytes 1048576 | tf_op jit(solution)/shard_map/all_to_all | solution.py:90
  472.6 8.2 %all-to-all-done.6 = bf16[16,32,512]{2,1,0:T(8,128)(2,1)S(1)} async-done(((bf16[16,32,512]{2,1,0:T(8,128)(2,1)}), bf16[16,32,512]{2,1,0:T(8,128)(2,1)S(1)}, u32[]{:S(2)}, u32[]{:S(2)}) %all-to-all-start.6) | async-done | bytes 524320 | tf_op jit(solution)/shard_map/all_to_all | solution.py:90
  480.8 6.2 all-to-all-start.7
  487.0 19.4 %all-to-all-done.7 = bf16[16,32,512]{2,1,0:T(8,128)(2,1)S(1)} async-done(((bf16[16,32,512]{2,1,0:T(8,128)(2,1)}), bf16[16,32,512]{2,1,0:T(8,128)(2,1)S(1)}, u32[]{:S(2)}, u32[]{:S(2)}) %all-to-all-start.7) | async-done | bytes 524320 | tf_op jit(solution)/shard_map/all_to_all | solution.py:93
  506.4 21.1 %all-gather.21.cloned.1.call-done = bf16[8192,512]{1,0:T(8,128)(2,1)} async-done(((bf16[512,512]{1,0:T(8,128)(2,1)}), bf16[8192,512]{1,0:T(8,128)(2,1)}) %all-gather.21.cloned.1.call-update) | async-done | bytes 8388624 | tf_op jit(solution)/shard_map/all_gather | solution.py:34
  527.5 78.5 %all-gather.23.cloned.1.call-done = bf16[8192,512]{1,0:T(8,128)(2,1)} async-done(((bf16[512,512]{1,0:T(8,128)(2,1)}), bf16[8192,512]{1,0:T(8,128)(2,1)}) %all-gather.23.cloned.1.call-update) | async-done | bytes 8388624 | tf_op jit(solution)/shard_map/all_gather | solution.py:34
  (55 shorter events, 70.9 us)
Async XLA Ops:
  6.5 66.3 %copy-start = (bf16[1,16,32,512]{3,2,1,0:T(8,128)(2,1)S(1)}, bf16[1,16,32,512]{3,2,1,0:T(8,128)(2,1)}, u32[]{:S(2)}) copy-start(bf16[1,16,32,512]{3,2,1,0:T(8,128)(2,1)} %param.31) | copy-start | bytes 1572868
  10.8 22.7 %all-to-all-start = ((f32[16,1,1,32,512]{4,3,2,1,0:T(8,128)}), f32[16,1,1,32,512]{4,3,2,1,0:T(8,128)S(1)}, u32[]{:S(2)}, u32[]{:S(2)}) async-start(f32[16,1,1,32,512]{4,3,2,1,0:T(8,128)} %broadcast_in_dim.35), calls=%async_computation | async-start | bytes 2097152 | tf_op jit(solution)/shard_map/all_to_all | solution.py:26
  34.6 32.5 %all-to-all-start.1 = ((f32[16,1,1,32,512]{4,3,2,1,0:T(8,128)}), f32[16,1,1,32,512]{4,3,2,1,0:T(8,128)S(1)}, u32[]{:S(2)}, u32[]{:S(2)}) async-start(f32[16,1,1,32,512]{4,3,2,1,0:T(8,128)} %stack.2), calls=%async_computation.1 | async-start | bytes 2097152 | tf_op jit(solution)/shard_map/all_to_all | solution.py:14
  42.7 120.1 %all-gather.13.cloned.1.call-start = ((), (), s32[]{:S(2)}) async-start(), calls=%async_computation.8 | async-start | bytes 8912896 | tf_op jit(solution)/shard_map/all_gather | solution.py:34
  67.1 5.8 copy-start.5
  67.1 39.0 %copy-start.1 = (bf16[16,1,32,512]{3,2,1,0:T(8,128)(2,1)S(1)}, bf16[16,1,32,512]{3,2,1,0:T(8,128)(2,1)}, u32[]{:S(2)}) copy-start(bf16[16,1,32,512]{3,2,1,0:T(8,128)(2,1)} %param.32) | copy-start | bytes 1572868
  72.1 169.3 %all-gather.15.cloned.1.call-start = ((), (), s32[]{:S(2)}) async-start(), calls=%async_computation.9 | async-start | bytes 8912896 | tf_op jit(solution)/shard_map/all_gather | solution.py:34
  74.3 42.6 %all-to-all-start.2 = ((bf16[16,32,512]{2,1,0:T(8,128)(2,1)}), bf16[16,32,512]{2,1,0:T(8,128)(2,1)}, u32[]{:S(2)}, u32[]{:S(2)}) async-start(bf16[16,32,512]{2,1,0:T(8,128)(2,1)} %gather_fusion), calls=%async_computation.2 | async-start | bytes 1048576 | tf_op jit(solution)/shard_map/all_to_all | solution.py:90
  116.9 25.5 %all-to-all-start.3 = ((bf16[16,32,512]{2,1,0:T(8,128)(2,1)}), bf16[16,32,512]{2,1,0:T(8,128)(2,1)}, u32[]{:S(2)}, u32[]{:S(2)}) async-start(bf16[16,32,512]{2,1,0:T(8,128)(2,1)} %gather_fusion.1), calls=%async_computation.3 | async-start | bytes 1048576 | tf_op jit(solution)/shard_map/all_to_all | solution.py:93
  123.0 223.4 %all-gather.17.cloned.1.call-start = ((), (), s32[]{:S(2)}) async-start(), calls=%async_computation.10 | async-start | bytes 8912896 | tf_op jit(solution)/shard_map/all_gather | solution.py:34
  250.0 7.9 %copy-start.4 = (s32[16]{0:T(128)S(1)}, s32[16]{0:T(128)}, u32[]{:S(2)}) copy-start(s32[16]{0:T(128)} %constant.202) | copy-start | bytes 196
  257.3 167.7 %all-gather.19.cloned.1.call-start = ((), (), s32[]{:S(2)}) async-start(), calls=%async_computation.11 | async-start | bytes 8912896 | tf_op jit(solution)/shard_map/all_gather | solution.py:34
  259.3 39.1 %all-to-all-start.4 = ((bf16[16,32,512]{2,1,0:T(8,128)(2,1)}), bf16[16,32,512]{2,1,0:T(8,128)(2,1)}, u32[]{:S(2)}, u32[]{:S(2)}) async-start(bf16[16,32,512]{2,1,0:T(8,128)(2,1)} %gather_fusion.2), calls=%async_computation.4 | async-start | bytes 1048576 | tf_op jit(solution)/shard_map/all_to_all | solution.py:90
  298.4 26.2 %all-to-all-start.5 = ((bf16[16,32,512]{2,1,0:T(8,128)(2,1)}), bf16[16,32,512]{2,1,0:T(8,128)(2,1)}, u32[]{:S(2)}, u32[]{:S(2)}) async-start(bf16[16,32,512]{2,1,0:T(8,128)(2,1)} %gather_fusion.3), calls=%async_computation.5 | async-start | bytes 1048576 | tf_op jit(solution)/shard_map/all_to_all | solution.py:93
  305.1 222.3 %all-gather.21.cloned.1.call-start = ((), (), s32[]{:S(2)}) async-start(), calls=%async_computation.12 | async-start | bytes 8912896 | tf_op jit(solution)/shard_map/all_gather | solution.py:34
  433.5 5.8 copy-start.3
  438.7 167.3 %all-gather.23.cloned.1.call-start = ((), (), s32[]{:S(2)}) async-start(), calls=%async_computation.13 | async-start | bytes 8912896 | tf_op jit(solution)/shard_map/all_gather | solution.py:34
  440.7 40.2 %all-to-all-start.6 = ((bf16[16,32,512]{2,1,0:T(8,128)(2,1)}), bf16[16,32,512]{2,1,0:T(8,128)(2,1)S(1)}, u32[]{:S(2)}, u32[]{:S(2)}) async-start(bf16[16,32,512]{2,1,0:T(8,128)(2,1)} %gather_fusion.4), calls=%async_computation.6 | async-start | bytes 1048576 | tf_op jit(solution)/shard_map/all_to_all | solution.py:90
  480.8 25.5 %all-to-all-start.7 = ((bf16[16,32,512]{2,1,0:T(8,128)(2,1)}), bf16[16,32,512]{2,1,0:T(8,128)(2,1)S(1)}, u32[]{:S(2)}, u32[]{:S(2)}) async-start(bf16[16,32,512]{2,1,0:T(8,128)(2,1)} %gather_fusion.5), calls=%async_computation.7 | async-start | bytes 1048576 | tf_op jit(solution)/shard_map/all_to_all | solution.py:93
  606.0 2.7 copy-start.2
Sparse Core Ops, SparseCore 0:
  72.2 90.5 all-gather.12
  165.2 76.1 all-gather.14
  257.4 88.9 all-gather.16
  348.7 76.1 all-gather.18
  438.8 88.6 all-gather.20
  529.8 76.1 all-gather.22
